TPU v7x, 512 devices: a whole 4x4x16 slice. The times are simulated.
512 devices in a mesh: section: 32 (over z, core), tensor: 16 (over x, y).
Axes of the slice: x: 4, y: 4, z: 16, core: 2. Of those that a mesh axis runs over, the one named last changes fastest.
Arguments:
- activations: bfloat16 [32, 512, 4096], P('section', None, 'tensor'), may hold values from -48 to 48
- gain: bfloat16 [32, 4096], P('section', 'tensor'), may hold values from 0.5 to 1.5
- w_query: bfloat16 [32, 4096, 4096], P('section', None, 'tensor'), may hold values from -0.0625 to 0.0625
- w_kv: bfloat16 [32, 1024, 4096], P('section', 'tensor'), may hold values from -1.8782524 to 1.8782524
- segments: int32 [32, 512], replicated, may hold values from 0 to 31, never falling along the last dimension, each value on 1 to 128 neighbouring positions
- pool: bfloat16 [64, 128, 4096], P('section', None, 'tensor'), may hold values from -48 to 48
- row_ids: int32 [32], replicated, may hold values from 0 to 63, as said below
- row_lengths: int32 [32], replicated, may hold values from 1 to 128, 512 in all
Outputs:
- after_first: bfloat16 [32, 512, 4096], P('section', None, 'tensor')
- after_second: bfloat16 [32, 512, 4096], P('section', None, 'tensor')
Inputs may be any that keep to these rules, and one draw needn't show every extreme that they name: `row_ids`: every block of 2 consecutive ids, the rows of one buffer host, is named at least once; ids may repeat.
All inputs are finite; a program needn't handle non-finite values.
Results may differ from a plain program's by a relative error of at most 0.01.
Values may be sent and summed in bfloat16 or wider, within the bound.
No kernel may reach another device: no remote copies, remote signals or barrier semaphores. Data moves between devices by JAX's collectives and lax.ppermute only.
A program may use at most 64 MiB of HBM per device.

v0:
```python
import jax
import jax.numpy as jnp
from jax import lax
from jax.sharding import PartitionSpec as P

D = 4096
HEADS = 32
KV_HEADS = 4
HEAD_DIM = 128
norm_eps = 1e-05
masked_score = -1e30


def partner_2(block, axis, distance):
    count = lax.axis_size(axis)
    route = []
    for low in range(count):
        high = low | 1 << distance
        if high != low and high < count:
            route += [(low, high), (high, low)]
    return lax.ppermute(block, axis, route)


def from_behind(block, axis, distance):
    devices = range(lax.axis_size(axis))
    route = [(i - distance, i) for i in devices if i - distance in devices]
    return lax.ppermute(block, axis, route)


def attend(inputs, gain_cols, query_weight, keyval_weight, seg_ids, tensor_index):
    row_count, col_count = inputs.shape
    wide_inputs = inputs.astype(jnp.float32)
    square_total = lax.psum(jnp.sum(wide_inputs * wide_inputs, axis=1), "tensor")
    row_scale = lax.rsqrt(square_total / D + norm_eps)
    normed = (wide_inputs * row_scale[:, None] * gain_cols.astype(jnp.float32)[None, :]).astype(
        jnp.bfloat16
    )
    part_cols = lax.all_gather(normed, "tensor", axis=1, tiled=True)
    query_part = jnp.dot(part_cols, query_weight, preferred_element_type=jnp.float32)
    keyval_part = lax.dot_general(
        keyval_weight, part_cols, (((1,), (1,)), ((), ())), preferred_element_type=jnp.float32
    )
    query = query_part.astype(jnp.bfloat16)
    keyval = keyval_part.astype(jnp.bfloat16)
    heads_here = query_weight.shape[1] // HEAD_DIM
    group_size = HEADS // KV_HEADS
    group_devices = group_size // heads_here
    head_block = keyval
    for bit_number in range(group_devices.bit_length() - 1):
        partner = partner_2(head_block, "tensor", bit_number)
        is_lower = tensor_index // (1 << bit_number) % 2 == 0
        head_block = jnp.where(
            is_lower,
            jnp.concatenate([head_block, partner], axis=0),
            jnp.concatenate([partner, head_block], axis=0),
        )
    keys_cols = head_block[:HEAD_DIM]
    values_cols = head_block[HEAD_DIM:]
    query_heads = query.reshape(row_count, heads_here, HEAD_DIM)
    scores = jnp.einsum(
        "rhd,ds->hrs", query_heads, keys_cols, preferred_element_type=jnp.float32
    ) * HEAD_DIM ** (-0.5)
    positions = jnp.arange(row_count, dtype=jnp.int32)
    allowed = (seg_ids[:, None] == seg_ids[None, :]) & (positions[None, :] <= positions[:, None])
    scores = jnp.where(allowed[None, :, :], scores, masked_score)
    weights = jax.nn.softmax(scores, axis=-1).astype(jnp.bfloat16)
    context = jnp.einsum("hrs,ds->rhd", weights, values_cols, preferred_element_type=jnp.float32)
    context = context.astype(jnp.bfloat16).reshape(row_count, col_count)
    return (wide_inputs + context.astype(jnp.float32)).astype(jnp.bfloat16)


def pick_rows(running, host_rows, source):
    flat_rows = host_rows.reshape(-1, host_rows.shape[2])
    inside = (source >= 0) & (source < flat_rows.shape[0])
    taken = jnp.take(flat_rows, jnp.clip(source, 0, flat_rows.shape[0] - 1), axis=0)
    return jnp.where(inside[:, None], taken, running)


def per_device(activations, gain, w_query, w_kv, segments, pool, row_ids, row_lengths):
    section_index = lax.axis_index("section")
    tensor_index = lax.axis_index("tensor")
    token_count = activations.shape[1]
    col_count = activations.shape[2]
    own_segments = lax.dynamic_index_in_dim(segments, section_index, 0, keepdims=False)
    after_first = attend(activations[0], gain[0], w_query[0], w_kv[0], own_segments, tensor_index)[
        None
    ]
    ends = jnp.cumsum(row_lengths)
    positions = jnp.arange(token_count, dtype=jnp.int32)
    slot = jnp.sum((positions[:, None] >= ends[None, :]).astype(jnp.int32), axis=1)
    slot_match = slot[:, None] == jnp.arange(row_ids.shape[0], dtype=jnp.int32)[None, :]
    slot_start = jnp.sum(jnp.where(slot_match, (ends - row_lengths)[None, :], 0), axis=1)
    slot_row = jnp.sum(jnp.where(slot_match, row_ids[None, :], 0), axis=1)
    source = slot_row * pool.shape[1] + positions - slot_start
    empty_rows = jnp.zeros((token_count, col_count), jnp.bfloat16)
    fresh = pick_rows(empty_rows, lax.all_gather(pool, "section", axis=0, tiled=True), source)
    handed = from_behind(after_first, "section", 1)
    second_inputs = jnp.where(section_index == 0, fresh[None], handed)
    prior_segments = lax.dynamic_index_in_dim(
        segments, jnp.maximum(section_index - 1, 0), 0, keepdims=False
    )
    second_segments = jnp.where(section_index == 0, slot, prior_segments)
    after_second = attend(
        second_inputs[0], gain[0], w_query[0], w_kv[0], second_segments, tensor_index
    )[None]
    return (after_first, after_second)


def solution(mesh):
    return jax.shard_map(
        per_device,
        mesh=mesh,
        in_specs=(
            P("section", None, "tensor"),
            P("section", "tensor"),
            P("section", None, "tensor"),
            P("section", "tensor", None),
            P(),
            P("section", None, "tensor"),
            P(),
            P(),
        ),
        out_specs=(P("section", None, "tensor"), P("section", None, "tensor")),
        check_vma=False,
    )
```

profile of v0, /device:TPU:2, one launch (start us, length us, event | category | flops | bytes accessed | tf_op | source)
XLA Modules:
  0.0 339.0 jit_solution(10043609363938623515)
XLA Ops:
  7.2 0.8 mul.92
  8.0 1.1 fusion.30
  9.1 34.8 %psum.14 = f32[512]{0:T(512)S(1)} all-reduce(f32[512]{0:T(512)S(1)} %fusion.30), channel_id=1, replica_groups=mesh['section'=32,'tensor'=16] {'tensor'}, use_global_device_ids=true, to_apply=%region_1.2 | all-reduce | flops 512 | bytes 4096 | tf_op jit(solution)/shard_map/psum | solution.py:33
  43.9 1.8 fusion.32
  46.6 0.7 copy.41
  48.2 0.7 select_reduce_fusion.1
  49.0 0.8 broadcast_select_fusion
  50.0 73.7 %all-gather.4.cloned.1.call-done = bf16[512,4096]{1,0:T(8,128)(2,1)} async-done(((bf16[512,256]{1,0:T(8,128)(2,1)}), bf16[512,4096]{1,0:T(8,128)(2,1)}) %all-gather.4.cloned.1.call-update) | async-done | bytes 4194320 | tf_op jit(solution)/shard_map/all_gather | solution.py:38
  123.7 3.7 %fusion.16 = bf16[64,512]{1,0:T(8,128)(2,1)S(1)} fusion(bf16[512,4096]{1,0:T(8,128)(2,1)} %all-gather.4.cloned.1.call-done, bf16[1,64,4096]{2,1,0:T(8,128)(2,1)} %param.11), kind=kOutput, calls=%fused_computation.23 | convolution fusion | flops 268468224 | bytes 4784128 | tf_op jit(solution)/shard_map/dot_general | solution.py:40
  127.4 2.2 collective-permute-start
  129.6 3.9 %collective-permute-done = bf16[64,512]{1,0:T(8,128)(2,1)S(1)} collective-permute-done((bf16[64,512]{1,0:T(8,128)(2,1)S(1)}, bf16[64,512]{1,0:T(8,128)(2,1)S(1)}, u32[]{:S(2)}, u32[]{:S(2)}) %collective-permute-start) | collective-permute-done | bytes 65568 | tf_op jit(solution)/shard_map/ppermute | solution.py:21
  133.6 3.4 %collective-permute-start.1 = (bf16[128,512]{1,0:T(8,128)(2,1)S(1)}, bf16[128,512]{1,0:T(8,128)(2,1)S(1)}, u32[]{:S(2)}, u32[]{:S(2)}) collective-permute-start(bf16[128,512]{1,0:T(8,128)(2,1)S(1)} %maximum_select_fusion.2), channel_id=1, source_target_pairs={{0,2},{2,0},{1,3},{3,1},{4,6},{6,4},{5,7},{7,5},{8,10},{10,8},{9,1... | collective-permute-start | bytes 393224 | tf_op jit(solution)/shard_map/ppermute | solution.py:21
  137.0 3.5 %fusion.8 = bf16[512,256]{0,1:T(8,128)(2,1)S(1)} fusion(bf16[512,4096]{1,0:T(8,128)(2,1)} %all-gather.4.cloned.1.call-done, bf16[1,4096,256]{2,1,0:T(8,128)(2,1)S(1)} %copy-done), kind=kOutput, calls=%fused_computation.15 | convolution fusion | flops 1073872896 | bytes 6553600 | tf_op jit(solution)/shard_map/dot_general | solution.py:39
  140.5 1.4 collective-permute-done.1
  142.0 0.9 fusion.63
  143.0 2.2 fusion.14
  145.4 0.8 fusion.33
  146.1 1.4 collective-permute-start.2
  147.6 52.3 %all-gather.6.cloned.1.call-done = bf16[64,128,256]{2,1,0:T(8,128)(2,1)} async-done(((bf16[2,128,256]{2,1,0:T(8,128)(2,1)}), bf16[64,128,256]{2,1,0:T(8,128)(2,1)}) %all-gather.6.cloned.1.call-update) | async-done | bytes 4194320 | tf_op jit(solution)/shard_map/all_gather | solution.py:96
  199.9 4.3 %gather_fusion = bf16[512,256]{1,0:T(8,128)(2,1)S(1)} fusion(bf16[8192,256]{1,0:T(8,128)(2,1)} %bitcast.129, s32[1024]{0:T(1024)S(1)} %pad_clamp_fusion), kind=kCustom, calls=%fused_computation | custom fusion | bytes 526336 | tf_op jit(solution)/shard_map/jit(_take)/gather | solution.py:75
  204.5 34.3 %psum.15 = f32[512]{0:T(512)S(1)} all-reduce(f32[512]{0:T(512)S(1)} %get-tuple-element.4), channel_id=1, replica_groups=mesh['section'=32,'tensor'=16] {'tensor'}, use_global_device_ids=true, to_apply=%region_9.10 | all-reduce | flops 512 | bytes 4096 | tf_op jit(solution)/shard_map/psum | solution.py:33
  238.8 0.8 fusion.36
  239.7 70.4 %all-gather.8.cloned.1.call-done = bf16[512,4096]{1,0:T(8,128)(2,1)} async-done(((bf16[512,256]{1,0:T(8,128)(2,1)}), bf16[512,4096]{1,0:T(8,128)(2,1)}) %all-gather.8.cloned.1.call-update) | async-done | bytes 4194320 | tf_op jit(solution)/shard_map/all_gather | solution.py:38
  310.1 3.7 %fusion.17 = bf16[64,512]{1,0:T(8,128)(2,1)S(1)} fusion(bf16[512,4096]{1,0:T(8,128)(2,1)} %all-gather.8.cloned.1.call-done, bf16[1,64,4096]{2,1,0:T(8,128)(2,1)S(1)} %copy-done.3), kind=kOutput, calls=%fused_computation.24 | convolution fusion | flops 268468224 | bytes 4784128 | tf_op jit(solution)/shard_map/dot_general | solution.py:40
  313.8 2.2 collective-permute-start.3
  316.2 3.8 %collective-permute-done.3 = bf16[64,512]{1,0:T(8,128)(2,1)S(1)} collective-permute-done((bf16[64,512]{1,0:T(8,128)(2,1)S(1)}, bf16[64,512]{1,0:T(8,128)(2,1)S(1)}, u32[]{:S(2)}, u32[]{:S(2)}) %collective-permute-start.3) | collective-permute-done | bytes 65568 | tf_op jit(solution)/shard_map/ppermute | solution.py:21
  320.0 3.6 %collective-permute-start.4 = (bf16[128,512]{1,0:T(8,128)(2,1)S(1)}, bf16[128,512]{1,0:T(8,128)(2,1)S(1)}, u32[]{:S(2)}, u32[]{:S(2)}) collective-permute-start(bf16[128,512]{1,0:T(8,128)(2,1)S(1)} %maximum_select_fusion.3), channel_id=1, source_target_pairs={{0,2},{2,0},{1,3},{3,1},{4,6},{6,4},{5,7},{7,5},{8,10},{10,8},{9,1... | collective-permute-start | bytes 393224 | tf_op jit(solution)/shard_map/ppermute | solution.py:21
  323.6 1.3 fusion.11
  324.9 3.4 %collective-permute-done.4 = bf16[128,512]{1,0:T(8,128)(2,1)S(1)} collective-permute-done((bf16[128,512]{1,0:T(8,128)(2,1)S(1)}, bf16[128,512]{1,0:T(8,128)(2,1)S(1)}, u32[]{:S(2)}, u32[]{:S(2)}) %collective-permute-start.4) | collective-permute-done | bytes 131104 | tf_op jit(solution)/shard_map/ppermute | solution.py:21
  328.5 0.9 fusion.64
  329.4 2.1 fusion.15
  331.7 0.8 fusion.37
  (39 shorter events, 3.1 us)
Async XLA Ops:
  7.2 129.8 %copy-start = (bf16[1,4096,256]{2,1,0:T(8,128)(2,1)S(1)}, bf16[1,4096,256]{2,1,0:T(8,128)(2,1)}, u32[]{:S(2)}) copy-start(bf16[1,4096,256]{2,1,0:T(8,128)(2,1)} %param.10) | copy-start | bytes 6291460
  7.2 116.5 %all-gather.4.cloned.1.call-start = ((), (), s32[]{:S(2)}) async-start(), calls=%async_computation | async-start | bytes 4456448 | tf_op jit(solution)/shard_map/all_gather | solution.py:38
  45.7 154.1 %all-gather.6.cloned.1.call-start = ((), (), s32[]{:S(2)}) async-start(), calls=%async_computation.1 | async-start | bytes 4325376 | tf_op jit(solution)/shard_map/all_gather | solution.py:96
  46.5 263.6 %all-gather.8.cloned.1.call-start = ((), (), s32[]{:S(2)}) async-start(), calls=%async_computation.2 | async-start | bytes 4456448 | tf_op jit(solution)/shard_map/all_gather | solution.py:38
  127.4 6.2 %collective-permute-start = (bf16[64,512]{1,0:T(8,128)(2,1)S(1)}, bf16[64,512]{1,0:T(8,128)(2,1)S(1)}, u32[]{:S(2)}, u32[]{:S(2)}) collective-permute-start(bf16[64,512]{1,0:T(8,128)(2,1)S(1)} %fusion.16), channel_id=1, source_target_pairs={{0,1},{1,0},{2,3},{3,2},{4,5},{5,4},{6,7},{7,6},{8,9},{9,8},{10,11... | collective-permute-start | bytes 196616 | tf_op jit(solution)/shard_map/ppermute | solution.py:21
  133.6 8.4 %collective-permute-start.1 = (bf16[128,512]{1,0:T(8,128)(2,1)S(1)}, bf16[128,512]{1,0:T(8,128)(2,1)S(1)}, u32[]{:S(2)}, u32[]{:S(2)}) collective-permute-start(bf16[128,512]{1,0:T(8,128)(2,1)S(1)} %maximum_select_fusion.2), channel_id=1, source_target_pairs={{0,2},{2,0},{1,3},{3,1},{4,6},{6,4},{5,7},{7,5},{8,10},{10,8},{9,1... | collective-permute-start | bytes 393224 | tf_op jit(solution)/shard_map/ppermute | solution.py:21
  140.5 1.5 copy-start.5
  143.0 2.4 copy-start.2
  146.1 163.9 %copy-start.3 = (bf16[1,64,4096]{2,1,0:T(8,128)(2,1)S(1)}, bf16[1,64,4096]{2,1,0:T(8,128)(2,1)}, u32[]{:S(2)}) copy-start(bf16[1,64,4096]{2,1,0:T(8,128)(2,1)} %param.11) | copy-start | bytes 1572868
  146.1 58.0 %collective-permute-start.2 = (bf16[1,512,256]{2,1,0:T(8,128)(2,1)}, bf16[1,512,256]{2,1,0:T(8,128)(2,1)S(1)}, u32[]{:S(2)}, u32[]{:S(2)}) collective-permute-start(bf16[1,512,256]{2,1,0:T(8,128)(2,1)} %fusion.33), channel_id=1, source_target_pairs={{0,16},{16,32},{32,48},{48,64},{64,80},{80,96},{96,112},{112,128},... | collective-permute-start | bytes 786440 | tf_op jit(solution)/shard_map/ppermute | solution.py:27
  310.1 13.5 %copy-start.1 = (bf16[512,4096]{1,0:T(8,128)(2,1)S(1)}, bf16[512,4096]{1,0:T(8,128)(2,1)}, u32[]{:S(2)}) copy-start(bf16[512,4096]{1,0:T(8,128)(2,1)} %all-gather.8.cloned.1.call-done) | copy-start | bytes 12582916
  313.8 6.2 %collective-permute-start.3 = (bf16[64,512]{1,0:T(8,128)(2,1)S(1)}, bf16[64,512]{1,0:T(8,128)(2,1)S(1)}, u32[]{:S(2)}, u32[]{:S(2)}) collective-permute-start(bf16[64,512]{1,0:T(8,128)(2,1)S(1)} %fusion.17), channel_id=1, source_target_pairs={{0,1},{1,0},{2,3},{3,2},{4,5},{5,4},{6,7},{7,6},{8,9},{9,8},{10,11... | collective-permute-start | bytes 196616 | tf_op jit(solution)/shard_map/ppermute | solution.py:21
  320.0 8.4 %collective-permute-start.4 = (bf16[128,512]{1,0:T(8,128)(2,1)S(1)}, bf16[128,512]{1,0:T(8,128)(2,1)S(1)}, u32[]{:S(2)}, u32[]{:S(2)}) collective-permute-start(bf16[128,512]{1,0:T(8,128)(2,1)S(1)} %maximum_select_fusion.3), channel_id=1, source_target_pairs={{0,2},{2,0},{1,3},{3,1},{4,6},{6,4},{5,7},{7,5},{8,10},{10,8},{9,1... | collective-permute-start | bytes 393224 | tf_op jit(solution)/shard_map/ppermute | solution.py:21
  324.9 3.5 %copy-start.4 = (bf16[512,256]{0,1:T(8,128)(2,1)}, bf16[512,256]{0,1:T(8,128)(2,1)S(1)}, u32[]{:S(2)}) copy-start(bf16[512,256]{0,1:T(8,128)(2,1)S(1)} %fusion.11) | copy-start | bytes 786436
Sparse Core Ops, SparseCore 0:
  45.9 77.8 all-gather.3
  125.8 73.9 all-gather.5
  239.8 70.2 all-gather.7
where the time goes:
time: 340 us; the launch traced here: 339 us
  waiting for transfers between devices  210 us (62%)
  blocking collectives  69.1 us (20%)
  matrix products  18.4 us (5%)
  between operations  14 us (4%)
  starting transfers between devices  12.9 us (4%)
  other arithmetic  9.48 us (3%)
  local copies, waits for them, and re-layouts  5.46 us (2%)
    all_gather x2, waiting for transfers between devices, attend(): part_cols = lax.all_gather(normed, 'tensor', axis=1, tiled=True)  144 us
    psum x2, blocking collectives, attend(): lax.psum(jnp.sum(wide_inputs * wide_inputs, axis=1), 'tensor')  69.1 us
    all_gather x1, waiting for transfers between devices, per_device(): lax.all_gather(pool, 'section', axis=0, tiled=True)  52.3 us
    ppermute x4, waiting for transfers between devices, partner_2(): return lax.ppermute(block, axis, route)  12.6 us
    ppermute x4, starting transfers between devices, partner_2(): return lax.ppermute(block, axis, route)  11.3 us
    dot_general x2, matrix products, attend(): lax.dot_general(keyval_weight, part_cols, (((1,), (1,)), ((), ())), prefe...  7.42 us
  transfers between devices with their start and end apart: 8, of which 7 were waited for; matrix products, arithmetic and copies ran while one was open for 6% of the time, Pallas kernels for 0%

commit v1 on v0

--- a/solution.py
+++ b/solution.py
@@ -30,7 +30,9 @@
 def attend(inputs, gain_cols, query_weight, keyval_weight, seg_ids, tensor_index):
     row_count, col_count = inputs.shape
     wide_inputs = inputs.astype(jnp.float32)
-    square_total = lax.psum(jnp.sum(wide_inputs * wide_inputs, axis=1), "tensor")
+    panel = jnp.sum(wide_inputs * wide_inputs, axis=1)
+    all_values = lax.all_gather(panel, axis_name="tensor")
+    square_total = jnp.sum(all_values, axis=0)
     row_scale = lax.rsqrt(square_total / D + norm_eps)
     normed = (wide_inputs * row_scale[:, None] * gain_cols.astype(jnp.float32)[None, :]).astype(
         jnp.bfloat16

time: 340 us -> 311 us (0.915)
  blocking collectives: 69.1 us -> 49.2 us
  waiting for transfers between devices: 210 us -> 201 us
    psum x2 -> x0, blocking collectives: 69.1 us -> none  [attend(): lax.psum(jnp.sum(wide_inputs * wide_inputs, axis=1), 'tensor')]
    all_gather x0 -> x2, blocking collectives: none -> 49.2 us  [attend(): all_values = lax.all_gather(panel, axis_name='tensor')]
    all_gather x2, waiting for transfers between devices: 144 us -> 136 us  [attend(): part_cols = lax.all_gather(normed, 'tensor', axis=1, tiled=True)]
  transfers between devices with their start and end apart: 8 -> 8, of which waited for: 7 -> 7; matrix products, arithmetic and copies ran while one was open for 6% -> 7% of each run, Pallas kernels for 0% -> 0%
where the time goes in v1:
time: 311 us
  waiting for transfers between devices  201 us (65%)
  blocking collectives  49.2 us (16%)
  matrix products  18.4 us (6%)
  between operations  14 us (5%)
  starting transfers between devices  12.9 us (4%)
  other arithmetic  9.56 us (3%)
  local copies, waits for them, and re-layouts  5.46 us (2%)
    all_gather x2, waiting for transfers between devices, attend(): part_cols = lax.all_gather(normed, 'tensor', axis=1, tiled=True)  136 us
    all_gather x1, waiting for transfers between devices, per_device(): lax.all_gather(pool, 'section', axis=0, tiled=True)  52.2 us
    all_gather x2, blocking collectives, attend(): all_values = lax.all_gather(panel, axis_name='tensor')  49.2 us
    ppermute x4, waiting for transfers between devices, partner_2(): return lax.ppermute(block, axis, route)  12.6 us
    ppermute x4, starting transfers between devices, partner_2(): return lax.ppermute(block, axis, route)  11.3 us
    dot_general x2, matrix products, attend(): lax.dot_general(keyval_weight, part_cols, (((1,), (1,)), ((), ())), prefe...  7.42 us
  transfers between devices with their start and end apart: 8, of which 7 were waited for; matrix products, arithmetic and copies ran while one was open for 7% of the time, Pallas kernels for 0%

profile of v1, /device:TPU:2, one launch (start us, length us, event | category | flops | bytes accessed | tf_op | source)
XLA Modules:
  0.0 310.9 jit_solution(14790415354478956893)
XLA Ops:
  7.2 0.8 mul.92
  8.0 1.1 fusion.30
  9.1 26.1 %all-gather.2 = f32[16,1,512]{2,1,0:T(1,128)S(1)} all-gather(f32[1,1,512]{2,1,0:T(1,128)S(1)} %bitcast.141), channel_id=2, replica_groups=mesh['section'=32,'tensor'=16] {'tensor'}, dimensions={0}, use_global_device_ids=true | all-gather | bytes 34816 | tf_op jit(solution)/shard_map/all_gather | solution.py:34
  35.3 1.8 fusion.32
  38.0 0.7 copy.41
  39.6 0.7 select_reduce_fusion.1
  40.4 0.8 broadcast_select_fusion
  41.4 68.3 %all-gather.8.cloned.1.call-done = bf16[512,4096]{1,0:T(8,128)(2,1)} async-done(((bf16[512,256]{1,0:T(8,128)(2,1)}), bf16[512,4096]{1,0:T(8,128)(2,1)}) %all-gather.8.cloned.1.call-update) | async-done | bytes 4194320 | tf_op jit(solution)/shard_map/all_gather | solution.py:40
  109.7 3.7 %fusion.16 = bf16[64,512]{1,0:T(8,128)(2,1)S(1)} fusion(bf16[512,4096]{1,0:T(8,128)(2,1)} %all-gather.8.cloned.1.call-done, bf16[1,64,4096]{2,1,0:T(8,128)(2,1)} %param.11), kind=kOutput, calls=%fused_computation.23 | convolution fusion | flops 268468224 | bytes 4784128 | tf_op jit(solution)/shard_map/dot_general | solution.py:42
  113.4 2.2 collective-permute-start
  115.6 3.9 %collective-permute-done = bf16[64,512]{1,0:T(8,128)(2,1)S(1)} collective-permute-done((bf16[64,512]{1,0:T(8,128)(2,1)S(1)}, bf16[64,512]{1,0:T(8,128)(2,1)S(1)}, u32[]{:S(2)}, u32[]{:S(2)}) %collective-permute-start) | collective-permute-done | bytes 65568 | tf_op jit(solution)/shard_map/ppermute | solution.py:21
  119.6 3.4 %collective-permute-start.1 = (bf16[128,512]{1,0:T(8,128)(2,1)S(1)}, bf16[128,512]{1,0:T(8,128)(2,1)S(1)}, u32[]{:S(2)}, u32[]{:S(2)}) collective-permute-start(bf16[128,512]{1,0:T(8,128)(2,1)S(1)} %maximum_select_fusion.2), channel_id=1, source_target_pairs={{0,2},{2,0},{1,3},{3,1},{4,6},{6,4},{5,7},{7,5},{8,10},{10,8},{9,1... | collective-permute-start | bytes 393224 | tf_op jit(solution)/shard_map/ppermute | solution.py:21
  123.0 3.5 %fusion.8 = bf16[512,256]{0,1:T(8,128)(2,1)S(1)} fusion(bf16[512,4096]{1,0:T(8,128)(2,1)} %all-gather.8.cloned.1.call-done, bf16[1,4096,256]{2,1,0:T(8,128)(2,1)S(1)} %copy-done), kind=kOutput, calls=%fused_computation.15 | convolution fusion | flops 1073872896 | bytes 6553600 | tf_op jit(solution)/shard_map/dot_general | solution.py:41
  126.5 1.4 collective-permute-done.1
  128.0 0.9 fusion.63
  129.0 2.2 fusion.14
  131.4 0.8 fusion.33
  132.1 1.4 collective-permute-start.2
  133.6 52.2 %all-gather.10.cloned.1.call-done = bf16[64,128,256]{2,1,0:T(8,128)(2,1)} async-done(((bf16[2,128,256]{2,1,0:T(8,128)(2,1)}), bf16[64,128,256]{2,1,0:T(8,128)(2,1)}) %all-gather.10.cloned.1.call-update) | async-done | bytes 4194320 | tf_op jit(solution)/shard_map/all_gather | solution.py:98
  185.9 4.3 %gather_fusion = bf16[512,256]{1,0:T(8,128)(2,1)S(1)} fusion(bf16[8192,256]{1,0:T(8,128)(2,1)} %bitcast.131, s32[1024]{0:T(1024)S(1)} %pad_clamp_fusion), kind=kCustom, calls=%fused_computation | custom fusion | bytes 526336 | tf_op jit(solution)/shard_map/jit(_take)/gather | solution.py:77
  190.5 23.0 %all-gather.3 = f32[16,1,512]{2,1,0:T(1,128)S(1)} all-gather(f32[1,1,512]{2,1,0:T(1,128)S(1)} %bitcast.140), channel_id=3, replica_groups=mesh['section'=32,'tensor'=16] {'tensor'}, dimensions={0}, use_global_device_ids=true | all-gather | bytes 34816 | tf_op jit(solution)/shard_map/all_gather | solution.py:34
  213.5 0.8 fusion.36
  214.4 67.5 %all-gather.12.cloned.1.call-done = bf16[512,4096]{1,0:T(8,128)(2,1)} async-done(((bf16[512,256]{1,0:T(8,128)(2,1)}), bf16[512,4096]{1,0:T(8,128)(2,1)}) %all-gather.12.cloned.1.call-update) | async-done | bytes 4194320 | tf_op jit(solution)/shard_map/all_gather | solution.py:40
  281.9 3.7 %fusion.17 = bf16[64,512]{1,0:T(8,128)(2,1)S(1)} fusion(bf16[512,4096]{1,0:T(8,128)(2,1)} %all-gather.12.cloned.1.call-done, bf16[1,64,4096]{2,1,0:T(8,128)(2,1)S(1)} %copy-done.3), kind=kOutput, calls=%fused_computation.24 | convolution fusion | flops 268468224 | bytes 4784128 | tf_op jit(solution)/shard_map/dot_general | solution.py:42
  285.6 2.2 collective-permute-start.3
  288.0 3.8 %collective-permute-done.3 = bf16[64,512]{1,0:T(8,128)(2,1)S(1)} collective-permute-done((bf16[64,512]{1,0:T(8,128)(2,1)S(1)}, bf16[64,512]{1,0:T(8,128)(2,1)S(1)}, u32[]{:S(2)}, u32[]{:S(2)}) %collective-permute-start.3) | collective-permute-done | bytes 65568 | tf_op jit(solution)/shard_map/ppermute | solution.py:21
  291.8 3.6 %collective-permute-start.4 = (bf16[128,512]{1,0:T(8,128)(2,1)S(1)}, bf16[128,512]{1,0:T(8,128)(2,1)S(1)}, u32[]{:S(2)}, u32[]{:S(2)}) collective-permute-start(bf16[128,512]{1,0:T(8,128)(2,1)S(1)} %maximum_select_fusion.3), channel_id=1, source_target_pairs={{0,2},{2,0},{1,3},{3,1},{4,6},{6,4},{5,7},{7,5},{8,10},{10,8},{9,1... | collective-permute-start | bytes 393224 | tf_op jit(solution)/shard_map/ppermute | solution.py:21
  295.4 1.3 fusion.11
  296.8 3.4 %collective-permute-done.4 = bf16[128,512]{1,0:T(8,128)(2,1)S(1)} collective-permute-done((bf16[128,512]{1,0:T(8,128)(2,1)S(1)}, bf16[128,512]{1,0:T(8,128)(2,1)S(1)}, u32[]{:S(2)}, u32[]{:S(2)}) %collective-permute-start.4) | collective-permute-done | bytes 131104 | tf_op jit(solution)/shard_map/ppermute | solution.py:21
  300.3 0.9 fusion.64
  301.2 2.1 fusion.15
  303.6 0.8 fusion.37
  (41 shorter events, 3.2 us)
Async XLA Ops:
  7.2 115.8 %copy-start = (bf16[1,4096,256]{2,1,0:T(8,128)(2,1)S(1)}, bf16[1,4096,256]{2,1,0:T(8,128)(2,1)}, u32[]{:S(2)}) copy-start(bf16[1,4096,256]{2,1,0:T(8,128)(2,1)} %param.10) | copy-start | bytes 6291460
  7.2 102.5 %all-gather.8.cloned.1.call-start = ((), (), s32[]{:S(2)}) async-start(), calls=%async_computation | async-start | bytes 4456448 | tf_op jit(solution)/shard_map/all_gather | solution.py:40
  37.2 148.7 %all-gather.10.cloned.1.call-start = ((), (), s32[]{:S(2)}) async-start(), calls=%async_computation.1 | async-start | bytes 4325376 | tf_op jit(solution)/shard_map/all_gather | solution.py:98
  37.9 244.0 %all-gather.12.cloned.1.call-start = ((), (), s32[]{:S(2)}) async-start(), calls=%async_computation.2 | async-start | bytes 4456448 | tf_op jit(solution)/shard_map/all_gather | solution.py:40
  113.4 6.2 %collective-permute-start = (bf16[64,512]{1,0:T(8,128)(2,1)S(1)}, bf16[64,512]{1,0:T(8,128)(2,1)S(1)}, u32[]{:S(2)}, u32[]{:S(2)}) collective-permute-start(bf16[64,512]{1,0:T(8,128)(2,1)S(1)} %fusion.16), channel_id=1, source_target_pairs={{0,1},{1,0},{2,3},{3,2},{4,5},{5,4},{6,7},{7,6},{8,9},{9,8},{10,11... | collective-permute-start | bytes 196616 | tf_op jit(solution)/shard_map/ppermute | solution.py:21
  119.6 8.4 %collective-permute-start.1 = (bf16[128,512]{1,0:T(8,128)(2,1)S(1)}, bf16[128,512]{1,0:T(8,128)(2,1)S(1)}, u32[]{:S(2)}, u32[]{:S(2)}) collective-permute-start(bf16[128,512]{1,0:T(8,128)(2,1)S(1)} %maximum_select_fusion.2), channel_id=1, source_target_pairs={{0,2},{2,0},{1,3},{3,1},{4,6},{6,4},{5,7},{7,5},{8,10},{10,8},{9,1... | collective-permute-start | bytes 393224 | tf_op jit(solution)/shard_map/ppermute | solution.py:21
  126.5 1.5 copy-start.5
  129.0 2.4 copy-start.2
  132.1 149.8 %copy-start.3 = (bf16[1,64,4096]{2,1,0:T(8,128)(2,1)S(1)}, bf16[1,64,4096]{2,1,0:T(8,128)(2,1)}, u32[]{:S(2)}) copy-start(bf16[1,64,4096]{2,1,0:T(8,128)(2,1)} %param.11) | copy-start | bytes 1572868
  132.1 58.0 %collective-permute-start.2 = (bf16[1,512,256]{2,1,0:T(8,128)(2,1)}, bf16[1,512,256]{2,1,0:T(8,128)(2,1)S(1)}, u32[]{:S(2)}, u32[]{:S(2)}) collective-permute-start(bf16[1,512,256]{2,1,0:T(8,128)(2,1)} %fusion.33), channel_id=1, source_target_pairs={{0,16},{16,32},{32,48},{48,64},{64,80},{80,96},{96,112},{112,128},... | collective-permute-start | bytes 786440 | tf_op jit(solution)/shard_map/ppermute | solution.py:27
  281.9 13.5 %copy-start.1 = (bf16[512,4096]{1,0:T(8,128)(2,1)S(1)}, bf16[512,4096]{1,0:T(8,128)(2,1)}, u32[]{:S(2)}) copy-start(bf16[512,4096]{1,0:T(8,128)(2,1)} %all-gather.12.cloned.1.call-done) | copy-start | bytes 12582916
  285.6 6.2 %collective-permute-start.3 = (bf16[64,512]{1,0:T(8,128)(2,1)S(1)}, bf16[64,512]{1,0:T(8,128)(2,1)S(1)}, u32[]{:S(2)}, u32[]{:S(2)}) collective-permute-start(bf16[64,512]{1,0:T(8,128)(2,1)S(1)} %fusion.17), channel_id=1, source_target_pairs={{0,1},{1,0},{2,3},{3,2},{4,5},{5,4},{6,7},{7,6},{8,9},{9,8},{10,11... | collective-permute-start | bytes 196616 | tf_op jit(solution)/shard_map/ppermute | solution.py:21
  291.8 8.4 %collective-permute-start.4 = (bf16[128,512]{1,0:T(8,128)(2,1)S(1)}, bf16[128,512]{1,0:T(8,128)(2,1)S(1)}, u32[]{:S(2)}, u32[]{:S(2)}) collective-permute-start(bf16[128,512]{1,0:T(8,128)(2,1)S(1)} %maximum_select_fusion.3), channel_id=1, source_target_pairs={{0,2},{2,0},{1,3},{3,1},{4,6},{6,4},{5,7},{7,5},{8,10},{10,8},{9,1... | collective-permute-start | bytes 393224 | tf_op jit(solution)/shard_map/ppermute | solution.py:21
  296.8 3.5 %copy-start.4 = (bf16[512,256]{0,1:T(8,128)(2,1)}, bf16[512,256]{0,1:T(8,128)(2,1)S(1)}, u32[]{:S(2)}) copy-start(bf16[512,256]{0,1:T(8,128)(2,1)S(1)} %fusion.11) | copy-start | bytes 786436
Sparse Core Ops, SparseCore 0:
  37.3 72.3 all-gather.7
  111.8 73.9 all-gather.9
  214.5 67.3 all-gather.11
